TPU v7x, 128 devices: a whole 4x4x4 slice. The times are simulated.
128 devices in a mesh: grp: 8 (over y_hi, z), gene: 16 (over y_lo, x, core).
Axes of the slice: x: 4, y: 4 (y_hi: 2, y_lo: 2; y = y_hi * 2 + y_lo), z: 4, core: 2. Of those that a mesh axis runs over, the one named last changes fastest.
Arguments:
- counts: int32 [2048, 15360], P('grp', 'gene'), may hold values from 0 to 12
- panels: int32 [15360], P('gene'), may hold values from 0 to 63
- membership: int32 [8, 256], P('grp'), may hold values from 0 to 3, never falling along the last dimension, each value on 1 to 128 neighbouring positions
- w_proj: bfloat16 [15360, 6400], P('gene'), may hold values from -0.0234375 to 0.0234375
- w_qkv_within: bfloat16 [1600, 32, 150], P(None, 'gene'), may hold values from -0.15625 to 0.15625
- w_out_within: bfloat16 [32, 50, 1600], P('gene'), may hold values from -0.4375 to 0.4375
- w_qkv_cross: bfloat16 [1600, 32, 150], P(None, 'gene'), may hold values from -0.15625 to 0.15625
- w_out_cross: bfloat16 [32, 50, 1600], P('gene'), may hold values from -0.4375 to 0.4375
- w_mean: bfloat16 [1600, 15360], P(None, 'gene'), may hold values from -0.25 to 0.25
- w_disp: bfloat16 [1600, 64], replicated, may hold values from -0.25 to 0.25
Outputs:
- cell_loss: float32 [2048], P('grp')
- grad_mean: float32 [1600, 15360], P('grp', 'gene')
- grad_disp: float32 [1600, 64], replicated
Inputs may be any that keep to these rules, and one draw needn't show every extreme that they name: `membership`: group numbers never fall along a row; a group has at most 128 cells.
All inputs are finite; a program needn't handle non-finite values.
Results may differ from a plain program's by a relative error of at most 0.00055.
Values may be sent and summed in bfloat16 or wider, within the bound.
A program may use at most 128 MiB of HBM per device.

v0:
```python
import jax
import jax.numpy as jnp
from jax import lax
from jax.sharding import PartitionSpec as P

EPS = 1e-06
FLOOR = 0.3
TARGET = 10000.0
DISP_BASE = 0.5


def rms_rows(values):
    return values * lax.rsqrt(jnp.mean(values * values, axis=-1, keepdims=True) + EPS)


def head_norm(values):
    return values * lax.rsqrt(jnp.maximum(jnp.mean(values * values, axis=-1, keepdims=True), FLOOR))


def split_heads(qkv, heads):
    qkv = qkv.reshape(qkv.shape[0], heads, 3, -1)
    query = head_norm(qkv[:, :, 0]).astype(jnp.bfloat16)
    keys = head_norm(qkv[:, :, 1]).astype(jnp.bfloat16)
    values = qkv[:, :, 2].astype(jnp.bfloat16)
    return (query, keys, values)


def within_cells(query, keys, values, modules):
    rows, heads, width = query.shape
    cells = rows // modules
    q_all = query.reshape(cells, modules, heads, width)
    k_all = keys.reshape(cells, modules, heads, width)
    v_all = values.reshape(cells, modules, heads, width)
    scores = jnp.einsum(
        "cmhd,cnhd->chmn", q_all, k_all, preferred_element_type=jnp.float32
    ) * width ** (-0.5)
    weights = jnp.exp(scores)
    probs = (weights / jnp.sum(weights, axis=-1, keepdims=True)).astype(jnp.bfloat16)
    mixed = jnp.einsum("chmn,cnhd->cmhd", probs, v_all, preferred_element_type=jnp.float32)
    return mixed.astype(jnp.bfloat16).reshape(rows, heads * width)


def across_cells(query, keys, values, groups, modules):
    rows, heads, width = query.shape
    cells = rows // modules
    q_all = query.reshape(cells, modules, heads, width)
    k_all = keys.reshape(cells, modules, heads, width)
    v_all = values.reshape(cells, modules, heads, width)
    scores = jnp.einsum(
        "cmhd,nmhd->mhcn", q_all, k_all, preferred_element_type=jnp.float32
    ) * width ** (-0.5)
    same = groups[:, None] == groups[None, :]
    weights = jnp.where(same[None, None], jnp.exp(scores), 0.0)
    probs = (weights / jnp.sum(weights, axis=-1, keepdims=True)).astype(jnp.bfloat16)
    mixed = jnp.einsum("mhcn,nmhd->cmhd", probs, v_all, preferred_element_type=jnp.float32)
    return mixed.astype(jnp.bfloat16).reshape(rows, heads * width)


def nb_terms(observed, rate, theta):
    total = theta + rate
    log_total = jnp.log(total)
    nll = -(
        lax.lgamma(observed + theta)
        - lax.lgamma(theta)
        - lax.lgamma(observed + 1.0)
        + theta * (jnp.log(theta) - log_total)
        + observed * (jnp.log(rate) - log_total)
    )
    d_rate = (theta + observed) / total - observed / rate
    d_theta = -(
        lax.digamma(observed + theta)
        - lax.digamma(theta)
        + jnp.log(theta)
        + 1.0
        - log_total
        - (theta + observed) / total
    )
    return (nll, d_rate, d_theta)


def shards(
    counts,
    panels,
    membership,
    w_proj,
    w_qkv_within,
    w_out_within,
    w_qkv_cross,
    w_out_cross,
    w_mean,
    w_disp,
):
    cells, genes_here = counts.shape
    width = w_qkv_within.shape[0]
    heads_here = w_qkv_within.shape[1]
    modules = w_proj.shape[1] // width
    gene_count = lax.axis_size("gene")
    genes_all = genes_here * gene_count
    rows = cells * modules
    share = rows // gene_count
    cell_share = cells // gene_count
    first = lax.axis_index("gene") * share
    observed = counts.astype(jnp.float32)
    library = 1.0 + lax.psum(jnp.sum(observed, axis=1), "gene")
    scaled = jnp.log1p(observed * (TARGET / library)[:, None]).astype(jnp.bfloat16)
    partial_value = jnp.dot(scaled, w_proj, preferred_element_type=jnp.float32).reshape(rows, width)
    tokens = lax.psum(partial_value, "gene")
    normed = rms_rows(tokens).astype(jnp.bfloat16)
    resid = lax.dynamic_slice_in_dim(tokens, first, share, 0)
    flat_within = w_qkv_within.reshape(width, -1)
    query, keys, values = split_heads(
        jnp.dot(normed, flat_within, preferred_element_type=jnp.float32), heads_here
    )
    mixed = within_cells(query, keys, values, modules)
    out_within = w_out_within.reshape(-1, width)
    block = mixed
    resid = resid + lax.psum_scatter(
        jnp.dot(block, out_within, preferred_element_type=jnp.float32),
        "gene",
        scatter_dimension=0,
        tiled=True,
    )
    flat_cross = w_qkv_cross.reshape(width, -1)
    qkv_cross = jnp.dot(
        lax.all_gather(rms_rows(resid).astype(jnp.bfloat16), "gene", axis=0, tiled=True),
        flat_cross,
        preferred_element_type=jnp.float32,
    )
    query, keys, values = split_heads(qkv_cross, heads_here)
    mixed = across_cells(query, keys, values, membership[0], modules)
    out_cross = w_out_cross.reshape(-1, width)
    block = mixed
    resid = resid + lax.psum_scatter(
        jnp.dot(block, out_cross, preferred_element_type=jnp.float32),
        "gene",
        scatter_dimension=0,
        tiled=True,
    )
    pooled = jnp.mean(resid.reshape(cell_share, modules, width), axis=1)
    hidden = lax.all_gather(rms_rows(pooled).astype(jnp.bfloat16), "gene", axis=0, tiled=True)
    panel_count = w_disp.shape[1]
    logit = jnp.dot(hidden, w_mean, preferred_element_type=jnp.float32)
    disp = jnp.dot(hidden, w_disp, preferred_element_type=jnp.float32)
    onehot = (panels[None, :] == jnp.arange(panel_count, dtype=jnp.int32)[:, None]).astype(
        jnp.float32
    )
    theta = jnp.dot(DISP_BASE + jax.nn.softplus(disp), onehot, precision=lax.Precision.HIGHEST)
    rate_scale = (library / genes_all)[:, None]
    rate = rate_scale * jax.nn.softplus(logit)
    nll, d_rate, d_theta = nb_terms(observed, rate, theta)
    norm_scale = (cells * lax.axis_size("grp")) ** (-0.5)
    d_logit = d_rate * rate_scale * jax.nn.sigmoid(logit) * norm_scale
    d_panel = jnp.dot(d_theta, onehot.T, precision=lax.Precision.HIGHEST)
    cell_part = jnp.sum(nll, axis=1)
    hidden_f = hidden.astype(jnp.float32)
    dims = (((0,), (0,)), ((), ()))
    cell_total = lax.psum(cell_part, "gene")
    d_disp = d_panel * jax.nn.sigmoid(disp) * norm_scale
    local_disp = lax.dot_general(hidden_f, d_disp, dims, precision=lax.Precision.HIGHEST)
    grad_disp = lax.psum(local_disp, ("grp", "gene"))
    cell_loss = cell_total / genes_all
    block = hidden_f
    grad_mean = lax.psum_scatter(
        lax.dot_general(block, d_logit, dims, precision=lax.Precision.HIGHEST),
        "grp",
        scatter_dimension=0,
        tiled=True,
    )
    return (cell_loss, grad_mean, grad_disp)


def solution(mesh):
    return jax.shard_map(
        shards,
        mesh=mesh,
        in_specs=(
            P("grp", "gene"),
            P("gene"),
            P("grp", None),
            P("gene", None),
            P(None, "gene", None),
            P("gene", None, None),
            P(None, "gene", None),
            P("gene", None, None),
            P(None, "gene"),
            P(),
        ),
        out_specs=(P("grp"), P("grp", "gene"), P()),
        check_vma=False,
    )
```

profile of v0, /device:TPU:0, one launch (start us, length us, event | category | flops | bytes accessed | tf_op | source)
XLA Modules:
  0.0 771.5 jit_solution(6979199559063120325)
XLA Ops:
  7.2 1.5 convert_reduce_fusion
  8.7 30.4 %psum.28 = f32[256]{0:T(256)S(1)} all-reduce(f32[256]{0:T(256)S(1)} %convert_reduce_fusion), channel_id=1, replica_groups=mesh['grp'=8,'gene'=16] {'gene'}, use_global_device_ids=true, to_apply=%region_1.0 | all-reduce | flops 256 | bytes 2048 | tf_op jit(solution)/shard_map/psum | solution.py:104
  39.2 11.2 %fusion.168 = f32[256,6400]{1,0:T(8,128)} fusion(bf16[960,6400]{1,0:T(8,128)(2,1)} %param.13, s32[256,960]{0,1:T(8,128)} %param.10, f32[256]{0:T(256)S(1)} %get-tuple-element.14), kind=kOutput, calls=%fused_computation.191 | convolution fusion | flops 3146465280 | bytes 19825664 | tf_op jit(solution)/shard_map/dot_general | solution.py:106
  50.4 8.7 %reshape.175 = f32[1024,1600]{1,0:T(8,128)} reshape(f32[256,6400]{1,0:T(8,128)} %fusion.168) | data formatting | bytes 13107200 | tf_op jit(solution)/shard_map/reshape | solution.py:106
  59.2 7.6 copy.115
  67.0 2.3 copy.116
  69.3 2.6 reshape.176
  71.8 2.4 dot_general.55
  75.0 1.9 reshape.178
  76.9 126.4 %all-reduce.3.cloned.1.call-done = f32[1024,1600]{0,1:T(8,128)} async-done(((f32[1024,1600]{0,1:T(8,128)}), f32[1024,1600]{0,1:T(8,128)}) %all-reduce.3.cloned.1.call-update) | async-done | bytes 6553616 | tf_op jit(solution)/shard_map/psum | solution.py:107
  203.3 3.5 multiply_reduce_fusion
  208.0 2.7 fusion.3
  213.8 2.3 copy.118
  216.1 2.5 copy.119
  218.6 3.9 fusion.165
  222.5 1.5 copy.122
  226.3 1.9 fusion.7
  228.2 1.3 copy.125
  230.9 4.9 fusion.246
  235.8 72.7 %reduce-scatter.10.cloned.1.call-done = f32[64,1600]{1,0:T(8,128)} async-done(((f32[1024,1600]{1,0:T(8,128)}), f32[64,1600]{1,0:T(8,128)}) %reduce-scatter.10.cloned.1.call-update) | async-done | bytes 409616
  308.5 2.2 copy.147
  310.7 1.7 multiply_reduce_fusion.1
  314.1 1.9 copy.128
  316.2 2.3 copy.129
  318.5 2.6 reshape.179
  321.1 2.4 dot_general.61
  324.3 1.8 reshape.181
  326.3 24.3 %all-gather.2.cloned.1.call-done = bf16[1024,1600]{1,0:T(8,128)(2,1)} async-done(((bf16[64,1600]{1,0:T(8,128)(2,1)}), bf16[1024,1600]{1,0:T(8,128)(2,1)}) %all-gather.2.cloned.1.call-update) | async-done | bytes 3276816 | tf_op jit(solution)/shard_map/all_gather | solution.py:125
  350.5 3.7 fusion
  356.1 2.4 copy.131
  358.8 2.3 copy.132
  362.1 2.0 copy.130
  364.1 1.7 multiply_convert_fusion.2
  365.9 1.8 multiply_convert_fusion.1
  371.4 4.9 fusion.247
  376.4 72.3 %reduce-scatter.12.cloned.1.call-done = f32[64,1600]{1,0:T(8,128)} async-done(((f32[1024,1600]{1,0:T(8,128)}), f32[64,1600]{1,0:T(8,128)}) %reduce-scatter.12.cloned.1.call-update) | async-done | bytes 409616
  448.7 2.2 copy.149
  450.9 2.4 add.116
  453.2 2.2 copy.140
  455.4 1.9 reshape.182
  458.8 19.2 %all_gather.7 = bf16[256,1600]{1,0:T(8,128)(2,1)S(1)} all-gather(bf16[16,1600]{1,0:T(8,128)(2,1)S(1)} %multiply_convert_fusion.6), channel_id=1, replica_groups=mesh['grp'=8,'gene'=16] {'gene'}, dimensions={0}, use_global_device_ids=true | all-gather | bytes 870400 | tf_op jit(solution)/shard_map/all_gather | solution.py:140
  479.5 19.0 %add_reduce_fusion = (f32[256]{0:T(256)S(1)}, f32[256,960]{0,1:T(8,128)S(1)}) fusion(s32[256,960]{0,1:T(8,128)S(1)} %copy-done.5, f32[256,960]{0,1:T(8,128)S(1)} %fusion.249, f32[256]{0:T(256)S(1)} %get-tuple-element.13, s32[960]{0:T(1024)S(1)} %copy-done.12, f32[256,64]{0,1:T(8,128)S(1)} %fusion.248), kind=kOutput, calls=%fused_computation.136 | convolution fusion | flops 231927552 | bytes 3020544 | tf_op jit(solution)/shard_map/dot_general | solution.py:147
  498.6 15.5 %fusion.9 = f32[256,64]{0,1:T(8,128)S(1)} fusion(f32[256,960]{0,1:T(8,128)S(1)} %get-tuple-element.18, s32[256,960]{0,1:T(8,128)S(1)} %copy-done.5, f32[256,960]{0,1:T(8,128)S(1)} %fusion.249, f32[256]{0:T(256)S(1)} %get-tuple-element.13, s32[960]{0:T(1024)S(1)} %copy-done.12, f32[256,64]{0,1:T(8,128)S(1)} %fusion.248), kind=kOutput, calls=%fused_computation.26 | convolution fusion | flops 229928960 | bytes 3085056 | tf_op jit(solution)/shard_map/dot_general | solution.py:153
  515.5 8.4 %fusion.107 = f32[1600,960]{1,0:T(8,128)} fusion(bf16[256,1600]{1,0:T(8,128)(2,1)} %copy-done.3, f32[256,960]{0,1:T(8,128)} %copy-done.13, s32[256,960]{0,1:T(8,128)S(1)} %copy-done.6, f32[256,960]{0,1:T(8,128)S(1)} %get-tuple-element.18, f32[256]{0:T(256)S(1)} %get-tuple-element.13), kind=kOutput, calls=%fused_computation.126 | convolution fusion | flops 4723261440 | bytes 9913344 | tf_op jit(solution)/shard_map/dot_general | solution.py:164
  523.9 29.0 %psum.30 = f32[256]{0:T(256)S(1)} all-reduce(f32[256]{0:T(256)S(1)} %neg.22), channel_id=1, replica_groups=mesh['grp'=8,'gene'=16] {'gene'}, use_global_device_ids=true, to_apply=%region_16.17 | all-reduce | flops 256 | bytes 2048 | tf_op jit(solution)/shard_map/psum | solution.py:157
  553.5 106.5 %all-reduce.5.cloned.1.call-done = f32[1600,64]{0,1:T(8,128)} async-done(((f32[1600,64]{0,1:T(8,128)}), f32[1600,64]{0,1:T(8,128)}) %all-reduce.5.cloned.1.call-update) | async-done | bytes 409616 | tf_op jit(solution)/shard_map/psum | solution.py:160
  660.0 102.6 %reduce-scatter.8.cloned.1.call-done = f32[200,960]{1,0:T(8,128)} async-done(((f32[1600,960]{1,0:T(8,128)}), f32[200,960]{1,0:T(8,128)}) %reduce-scatter.8.cloned.1.call-update) | async-done | bytes 768016 | tf_op jit(solution)/shard_map/reduce_scatter | solution.py:163
  762.6 1.8 copy.168
  (76 shorter events, 23.6 us)
Async XLA Ops:
  7.2 470.8 %copy-start = (bf16[1600,960]{0,1:T(8,128)(2,1)S(1)}, bf16[1600,960]{0,1:T(8,128)(2,1)}, u32[]{:S(2)}) copy-start(bf16[1600,960]{0,1:T(8,128)(2,1)} %param.18) | copy-start | bytes 9216004
  7.2 196.1 %all-reduce.3.cloned.1.call-start = ((), (), s32[]{:S(2)}) async-start(), calls=%async_computation.3 | async-start | bytes 13107200 | tf_op jit(solution)/shard_map/psum | solution.py:107
  66.7 7.5 copy-start.8
  66.8 241.7 %reduce-scatter.10.cloned.1.call-start = ((), (), s32[]{:S(2)}) async-start(), calls=%async_computation.7 | async-start | bytes 7241728
  203.3 4.7 copy-start.2
  235.7 114.8 %all-gather.2.cloned.1.call-start = ((), (), s32[]{:S(2)}) async-start(), calls=%async_computation.4 | async-start | bytes 3620864 | tf_op jit(solution)/shard_map/all_gather | solution.py:125
  312.4 0.9 copy-start.4
  315.9 7.6 copy-start.9
  316.0 132.7 %reduce-scatter.12.cloned.1.call-start = ((), (), s32[]{:S(2)}) async-start(), calls=%async_computation.8 | async-start | bytes 7241728
  318.5 7.6 copy-start.11
  365.8 2.5 copy-start.7
  376.3 283.7 %all-reduce.5.cloned.1.call-start = ((), (), s32[]{:S(2)}) async-start(), calls=%async_computation.6 | async-start | bytes 851968 | tf_op jit(solution)/shard_map/psum | solution.py:160
  458.8 20.3 %copy-start.10 = (bf16[1600,64]{0,1:T(8,128)(2,1)S(1)}, bf16[1600,64]{0,1:T(8,128)(2,1)}, u32[]{:S(2)}) copy-start(bf16[1600,64]{0,1:T(8,128)(2,1)} %param.19) | copy-start | bytes 614404
  478.0 36.1 %copy-start.3 = (bf16[256,1600]{1,0:T(8,128)(2,1)}, bf16[256,1600]{1,0:T(8,128)(2,1)S(1)}, u32[]{:S(2)}) copy-start(bf16[256,1600]{1,0:T(8,128)(2,1)S(1)} %all_gather.7) | copy-start | bytes 2457604
  478.0 1.5 copy-start.5
  478.0 1.5 copy-start.12
  479.1 19.4 %copy-start.13 = (f32[256,960]{0,1:T(8,128)}, f32[256,960]{0,1:T(8,128)S(1)}, u32[]{:S(2)}) copy-start(f32[256,960]{0,1:T(8,128)S(1)} %fusion.249) | copy-start | bytes 2949124
  498.6 16.9 %copy-start.6 = (s32[256,960]{0,1:T(8,128)S(1)}, s32[256,960]{0,1:T(8,128)}, u32[]{:S(2)}) copy-start(s32[256,960]{0,1:T(8,128)} %param.10) | copy-start | bytes 2949124
  515.4 247.2 %reduce-scatter.8.cloned.1.call-start = ((), (), s32[]{:S(2)}) async-start(), calls=%async_computation.5 | async-start | bytes 7372800 | tf_op jit(solution)/shard_map/reduce_scatter | solution.py:163
  523.9 240.6 %copy-start.1 = (bf16[1600,960]{0,1:T(8,128)(2,1)S(1)}, bf16[1600,960]{0,1:T(8,128)(2,1)}, u32[]{:S(2)}) copy-start(bf16[1600,960]{0,1:T(8,128)(2,1)} %param.18) | copy-start | bytes 9216004
Sparse Core Ops, SparseCore 0:
  66.9 136.3 all-reduce.2
  235.9 72.5 reduce-scatter.9
  316.1 34.4 all-gather.1
  376.5 72.1 reduce-scatter.11
  515.5 144.4 all-reduce.4
  664.3 98.2 reduce-scatter.7
where the time goes:
time: 777 us; the launch traced here: 772 us
  waiting for transfers between devices  505 us (65%)
  matrix products  80.1 us (10%)
  blocking collectives  78.6 us (10%)
  local copies, waits for them, and re-layouts  74.7 us (10%)
  other arithmetic  17.9 us (2%)
  between operations  14.7 us (2%)
    unnamed x8, waiting for transfers between devices  145 us
    psum x1, waiting for transfers between devices, shards(): tokens = lax.psum(partial_value, 'gene')  126 us
    psum x1, waiting for transfers between devices, shards(): grad_disp = lax.psum(local_disp, ('grp', 'gene'))  107 us
    reduce_scatter x1, waiting for transfers between devices, shards(): lax.psum_scatter(lax.dot_general(block, d_logit, dims, precision=lax.Prec...  103 us
    psum x1, blocking collectives, shards(): library = 1.0 + lax.psum(jnp.sum(observed, axis=1), 'gene')  30.4 us
    psum x1, blocking collectives, shards(): cell_total = lax.psum(cell_part, 'gene')  29 us
    all_gather x1, waiting for transfers between devices, shards(): lax.all_gather(rms_rows(resid).astype(jnp.bfloat16), 'gene', axis=0, tile...  24.3 us
    all_gather x1, blocking collectives, shards(): lax.all_gather(rms_rows(pooled).astype(jnp.bfloat16), 'gene', axis=0, til...  19.2 us
  transfers between devices with their start and end apart: 6, of which 6 were waited for; matrix products, arithmetic and copies ran while one was open for 4% of the time, Pallas kernels for 0%

commit v1 on v0

--- a/solution.py
+++ b/solution.py
@@ -157,7 +157,9 @@
     cell_total = lax.psum(cell_part, "gene")
     d_disp = d_panel * jax.nn.sigmoid(disp) * norm_scale
     local_disp = lax.dot_general(hidden_f, d_disp, dims, precision=lax.Precision.HIGHEST)
-    grad_disp = lax.psum(local_disp, ("grp", "gene"))
+    grad_disp = local_disp
+    for b in ("gene", "grp"):
+        grad_disp = lax.psum(grad_disp, b)
     cell_loss = cell_total / genes_all
     block = hidden_f
     grad_mean = lax.psum_scatter(

time: 777 us -> 838 us (1.079)
  waiting for transfers between devices: 505 us -> 566 us
    psum x1 -> x2, waiting for transfers between devices: 107 us -> 167 us  [shards(): grad_disp = lax.psum(grad_disp, b)]
    unnamed x8 -> x9, waiting for transfers between devices: 145 us -> 145 us
  transfers between devices with their start and end apart: 6 -> 7, of which waited for: 6 -> 7; matrix products, arithmetic and copies ran while one was open for 4% -> 3% of each run, Pallas kernels for 0% -> 0%
where the time goes in v1:
time: 838 us; the launch traced here: 832 us
  waiting for transfers between devices  566 us (68%)
  matrix products  80.1 us (10%)
  blocking collectives  77.8 us (9%)
  local copies, waits for them, and re-layouts  74.7 us (9%)
  other arithmetic  17.9 us (2%)
  between operations  14.7 us (2%)
    psum x2, waiting for transfers between devices, shards(): grad_disp = lax.psum(grad_disp, b)  167 us
    unnamed x9, waiting for transfers between devices  145 us
    psum x1, waiting for transfers between devices, shards(): tokens = lax.psum(partial_value, 'gene')  126 us
    reduce_scatter x1, waiting for transfers between devices, shards(): lax.psum_scatter(lax.dot_general(block, d_logit, dims, precision=lax.Prec...  103 us
    psum x1, blocking collectives, shards(): library = 1.0 + lax.psum(jnp.sum(observed, axis=1), 'gene')  30.4 us
    psum x1, blocking collectives, shards(): cell_total = lax.psum(cell_part, 'gene')  28.1 us
    all_gather x1, waiting for transfers between devices, shards(): lax.all_gather(rms_rows(resid).astype(jnp.bfloat16), 'gene', axis=0, tile...  24.3 us
    all_gather x1, blocking collectives, shards(): lax.all_gather(rms_rows(pooled).astype(jnp.bfloat16), 'gene', axis=0, til...  19.2 us
  transfers between devices with their start and end apart: 7, of which 7 were waited for; matrix products, arithmetic and copies ran while one was open for 3% of the time, Pallas kernels for 0%

profile of v1, /device:TPU:0, one launch (start us, length us, event | category | flops | bytes accessed | tf_op | source)
XLA Modules:
  0.0 831.8 jit_solution(10526446550214184352)
XLA Ops:
  7.2 1.5 convert_reduce_fusion
  8.7 30.4 %psum.35 = f32[256]{0:T(256)S(1)} all-reduce(f32[256]{0:T(256)S(1)} %convert_reduce_fusion), channel_id=1, replica_groups=mesh['grp'=8,'gene'=16] {'gene'}, use_global_device_ids=true, to_apply=%region_1.0 | all-reduce | flops 256 | bytes 2048 | tf_op jit(solution)/shard_map/psum | solution.py:104
  39.2 11.2 %fusion.168 = f32[256,6400]{1,0:T(8,128)} fusion(bf16[960,6400]{1,0:T(8,128)(2,1)} %param.13, s32[256,960]{0,1:T(8,128)} %param.10, f32[256]{0:T(256)S(1)} %get-tuple-element.14), kind=kOutput, calls=%fused_computation.191 | convolution fusion | flops 3146465280 | bytes 19825664 | tf_op jit(solution)/shard_map/dot_general | solution.py:106
  50.4 8.7 %reshape.175 = f32[1024,1600]{1,0:T(8,128)} reshape(f32[256,6400]{1,0:T(8,128)} %fusion.168) | data formatting | bytes 13107200 | tf_op jit(solution)/shard_map/reshape | solution.py:106
  59.2 7.6 copy.115
  67.0 2.3 copy.116
  69.3 2.6 reshape.176
  71.8 2.4 dot_general.55
  75.0 1.9 reshape.178
  76.9 126.4 %all-reduce.4.cloned.1.call-done = f32[1024,1600]{0,1:T(8,128)} async-done(((f32[1024,1600]{0,1:T(8,128)}), f32[1024,1600]{0,1:T(8,128)}) %all-reduce.4.cloned.1.call-update) | async-done | bytes 6553616 | tf_op jit(solution)/shard_map/psum | solution.py:107
  203.3 3.5 multiply_reduce_fusion
  208.0 2.7 fusion.3
  213.8 2.3 copy.118
  216.1 2.5 copy.119
  218.6 3.9 fusion.165
  222.5 1.5 copy.122
  226.3 1.9 fusion.7
  230.9 4.9 fusion.246
  235.8 72.7 %reduce-scatter.10.cloned.1.call-done = f32[64,1600]{1,0:T(8,128)} async-done(((f32[1024,1600]{1,0:T(8,128)}), f32[64,1600]{1,0:T(8,128)}) %reduce-scatter.10.cloned.1.call-update) | async-done | bytes 409616
  308.5 2.2 copy.147
  310.7 1.7 multiply_reduce_fusion.1
  314.1 1.9 copy.128
  316.2 2.3 copy.129
  318.5 2.6 reshape.179
  321.1 2.4 dot_general.61
  324.3 1.8 reshape.181
  326.3 24.3 %all-gather.2.cloned.1.call-done = bf16[1024,1600]{1,0:T(8,128)(2,1)} async-done(((bf16[64,1600]{1,0:T(8,128)(2,1)}), bf16[1024,1600]{1,0:T(8,128)(2,1)}) %all-gather.2.cloned.1.call-update) | async-done | bytes 3276816 | tf_op jit(solution)/shard_map/all_gather | solution.py:125
  350.5 3.7 fusion
  356.1 2.4 copy.131
  358.8 2.3 copy.132
  362.1 2.0 copy.130
  364.1 1.7 multiply_convert_fusion.2
  365.9 1.8 multiply_convert_fusion.1
  371.4 4.9 fusion.247
  376.4 72.3 %reduce-scatter.12.cloned.1.call-done = f32[64,1600]{1,0:T(8,128)} async-done(((f32[1024,1600]{1,0:T(8,128)}), f32[64,1600]{1,0:T(8,128)}) %reduce-scatter.12.cloned.1.call-update) | async-done | bytes 409616
  448.7 2.2 copy.149
  450.9 2.4 add.118
  453.2 2.2 copy.140
  455.4 1.9 reshape.182
  458.8 19.2 %all_gather.7 = bf16[256,1600]{1,0:T(8,128)(2,1)S(1)} all-gather(bf16[16,1600]{1,0:T(8,128)(2,1)S(1)} %multiply_convert_fusion.6), channel_id=1, replica_groups=mesh['grp'=8,'gene'=16] {'gene'}, dimensions={0}, use_global_device_ids=true | all-gather | bytes 870400 | tf_op jit(solution)/shard_map/all_gather | solution.py:140
  479.5 19.0 %add_reduce_fusion = (f32[256]{0:T(256)S(1)}, f32[256,960]{0,1:T(8,128)S(1)}) fusion(s32[256,960]{0,1:T(8,128)S(1)} %copy-done.5, f32[256,960]{0,1:T(8,128)S(1)} %fusion.249, f32[256]{0:T(256)S(1)} %get-tuple-element.13, s32[960]{0:T(1024)S(1)} %copy-done.12, f32[256,64]{0,1:T(8,128)S(1)} %fusion.248), kind=kOutput, calls=%fused_computation.136 | convolution fusion | flops 231927552 | bytes 3020544 | tf_op jit(solution)/shard_map/dot_general | solution.py:147
  498.6 15.5 %fusion.9 = f32[256,64]{0,1:T(8,128)S(1)} fusion(f32[256,960]{0,1:T(8,128)S(1)} %get-tuple-element.18, s32[256,960]{0,1:T(8,128)S(1)} %copy-done.5, f32[256,960]{0,1:T(8,128)S(1)} %fusion.249, f32[256]{0:T(256)S(1)} %get-tuple-element.13, s32[960]{0:T(1024)S(1)} %copy-done.12, f32[256,64]{0,1:T(8,128)S(1)} %fusion.248), kind=kOutput, calls=%fused_computation.26 | convolution fusion | flops 229928960 | bytes 3085056 | tf_op jit(solution)/shard_map/dot_general | solution.py:153
  515.5 114.7 %all-reduce.6.cloned.1.call-done = f32[1600,64]{0,1:T(8,128)} async-done(((f32[1600,64]{0,1:T(8,128)}), f32[1600,64]{0,1:T(8,128)}) %all-reduce.6.cloned.1.call-update) | async-done | bytes 409616 | tf_op jit(solution)/shard_map/psum | solution.py:162
  630.3 8.4 %fusion.107 = f32[1600,960]{1,0:T(8,128)} fusion(bf16[256,1600]{1,0:T(8,128)(2,1)} %copy-done.3, f32[256,960]{0,1:T(8,128)} %copy-done.13, s32[256,960]{0,1:T(8,128)S(1)} %copy-done.6, f32[256,960]{0,1:T(8,128)S(1)} %get-tuple-element.18, f32[256]{0:T(256)S(1)} %get-tuple-element.13), kind=kOutput, calls=%fused_computation.126 | convolution fusion | flops 4723261440 | bytes 9913344 | tf_op jit(solution)/shard_map/dot_general | solution.py:166
  638.7 28.1 %psum.37 = f32[256]{0:T(256)S(1)} all-reduce(f32[256]{0:T(256)S(1)} %neg.22), channel_id=1, replica_groups=mesh['grp'=8,'gene'=16] {'gene'}, use_global_device_ids=true, to_apply=%region_16.17 | all-reduce | flops 256 | bytes 2048 | tf_op jit(solution)/shard_map/psum | solution.py:157
  667.4 52.5 %all-reduce.8.cloned.1.call-done = f32[1600,64]{0,1:T(8,128)} async-done(((f32[1600,64]{0,1:T(8,128)}), f32[1600,64]{0,1:T(8,128)}) %all-reduce.8.cloned.1.call-update) | async-done | bytes 409616 | tf_op jit(solution)/shard_map/psum | solution.py:162
  719.9 102.9 %reduce-scatter.8.cloned.1.call-done = f32[200,960]{1,0:T(8,128)} async-done(((f32[1600,960]{1,0:T(8,128)}), f32[200,960]{1,0:T(8,128)}) %reduce-scatter.8.cloned.1.call-update) | async-done | bytes 768016 | tf_op jit(solution)/shard_map/reduce_scatter | solution.py:165
  822.8 1.8 copy.169
  (79 shorter events, 25.0 us)
Async XLA Ops:
  7.2 470.8 %copy-start = (bf16[1600,960]{0,1:T(8,128)(2,1)S(1)}, bf16[1600,960]{0,1:T(8,128)(2,1)}, u32[]{:S(2)}) copy-start(bf16[1600,960]{0,1:T(8,128)(2,1)} %param.18) | copy-start | bytes 9216004
  7.2 196.1 %all-reduce.4.cloned.1.call-start = ((), (), s32[]{:S(2)}) async-start(), calls=%async_computation.3 | async-start | bytes 13107200 | tf_op jit(solution)/shard_map/psum | solution.py:107
  66.7 7.5 copy-start.8
  66.8 241.7 %reduce-scatter.10.cloned.1.call-start = ((), (), s32[]{:S(2)}) async-start(), calls=%async_computation.8 | async-start | bytes 7241728
  203.3 4.7 copy-start.2
  235.7 114.8 %all-gather.2.cloned.1.call-start = ((), (), s32[]{:S(2)}) async-start(), calls=%async_computation.4 | async-start | bytes 3620864 | tf_op jit(solution)/shard_map/all_gather | solution.py:125
  312.4 0.9 copy-start.4
  315.9 7.6 copy-start.9
  316.0 132.7 %reduce-scatter.12.cloned.1.call-start = ((), (), s32[]{:S(2)}) async-start(), calls=%async_computation.9 | async-start | bytes 7241728
  318.5 7.6 copy-start.11
  365.8 2.5 copy-start.7
  376.3 253.9 %all-reduce.6.cloned.1.call-start = ((), (), s32[]{:S(2)}) async-start(), calls=%async_computation.6 | async-start | bytes 851968 | tf_op jit(solution)/shard_map/psum | solution.py:162
  458.8 20.3 %copy-start.10 = (bf16[1600,64]{0,1:T(8,128)(2,1)S(1)}, bf16[1600,64]{0,1:T(8,128)(2,1)}, u32[]{:S(2)}) copy-start(bf16[1600,64]{0,1:T(8,128)(2,1)} %param.19) | copy-start | bytes 614404
  478.0 36.1 %copy-start.3 = (bf16[256,1600]{1,0:T(8,128)(2,1)}, bf16[256,1600]{1,0:T(8,128)(2,1)S(1)}, u32[]{:S(2)}) copy-start(bf16[256,1600]{1,0:T(8,128)(2,1)S(1)} %all_gather.7) | copy-start | bytes 2457604
  478.0 1.5 copy-start.5
  478.0 1.5 copy-start.12
  479.1 19.4 %copy-start.13 = (f32[256,960]{0,1:T(8,128)}, f32[256,960]{0,1:T(8,128)S(1)}, u32[]{:S(2)}) copy-start(f32[256,960]{0,1:T(8,128)S(1)} %fusion.249) | copy-start | bytes 2949124
  498.6 131.7 %copy-start.6 = (s32[256,960]{0,1:T(8,128)S(1)}, s32[256,960]{0,1:T(8,128)}, u32[]{:S(2)}) copy-start(s32[256,960]{0,1:T(8,128)} %param.10) | copy-start | bytes 2949124
  515.4 204.5 %all-reduce.8.cloned.1.call-start = ((), (), s32[]{:S(2)}) async-start(), calls=%async_computation.7 | async-start | bytes 851968 | tf_op jit(solution)/shard_map/psum | solution.py:162
  630.2 192.6 %reduce-scatter.8.cloned.1.call-start = ((), (), s32[]{:S(2)}) async-start(), calls=%async_computation.5 | async-start | bytes 7372800 | tf_op jit(solution)/shard_map/reduce_scatter | solution.py:165
  638.7 185.9 %copy-start.1 = (bf16[1600,960]{0,1:T(8,128)(2,1)S(1)}, bf16[1600,960]{0,1:T(8,128)(2,1)}, u32[]{:S(2)}) copy-start(bf16[1600,960]{0,1:T(8,128)(2,1)} %param.18) | copy-start | bytes 9216004
Sparse Core Ops, SparseCore 0:
  66.9 136.3 all-reduce.3
  235.9 72.5 reduce-scatter.9
  316.1 34.4 all-gather.1
  376.5 72.1 reduce-scatter.11
  515.5 114.6 all-reduce.5
  632.5 87.3 all-reduce.7
  724.4 98.4 reduce-scatter.7
